TPU v7x, 32 devices: a whole 2x2x4 slice. The times are simulated.
32 devices in a mesh: grp: 4 (over y, x), dev: 8 (over z, core).
Axes of the slice: x: 2, y: 2, z: 4, core: 2. Of those that a mesh axis runs over, the one named last changes fastest.
Arguments:
- points: float32 [64, 49152], P(None, 'dev'), may hold values from -6 to 6
- weights: float32 [49152, 128], P('dev'), may hold values from -4 to 4
- proj: float32 [256, 49152], P(None, 'dev'), may hold values from -0.078125 to 0.078125
- fetch_table: int32 [3, 8, 8, 2], P(None, 'dev'), may hold values from 0 to 11, as said below
- near_list: int32 [96, 16], P('dev'), may hold values from 0 to 15, as said below
- far_list: int32 [96, 8], P('dev'), may hold values from 0 to 7, as said below
- skel_idx: int32 [8, 256], P('dev'), may hold values from 0 to 6143, as said below
Outputs:
- potential: float32 [49152, 128], P('dev')
Inputs may be any that keep to these rules, and one draw needn't show every extreme that they name: Entries of fetch_table[r, d, e] are distinct local leaf numbers of column e. `near_list`: the 16 slots of one target leaf are distinct. `far_list`: the 8 nodes of one target leaf are distinct, and one of them is node (c + 1) mod 8 for the leaf's column c. `skel_idx`: the 256 skeleton points of one node are distinct.
All inputs are finite; a program needn't handle non-finite values.
Results may differ from a plain program's by a relative error of at most 0.0003.
Values sent between devices are 32-bit elements; how exact they have to be, the bound alone decides.
No kernel may reach another device: no remote copies, remote signals or barrier semaphores. Data moves between devices by JAX's collectives and lax.ppermute only.
A program may use at most 192 MiB of HBM per device.

v0:
```python
import jax
import jax.numpy as jnp
from jax import lax
from jax.sharding import PartitionSpec as P


def kernel_sum(target, sources, values):
    high = lax.Precision.HIGHEST
    inner = jnp.einsum("dt,jds->tjs", target, sources, precision=high)
    target_norm = jnp.sum(target * target, axis=0)
    source_norm = jnp.sum(sources * sources, axis=1)
    distance = target_norm[:, None, None] + source_norm[None] - 2.0 * inner
    kernel = jnp.exp(-distance * (2.0 / target.shape[0]))
    return jnp.einsum("tjs,jsw->tw", kernel, values, precision=high)


def on_device(points, weights, proj, fetch_table, near_list, far_list, skel_idx):
    features, column_points = points.shape
    columns = weights.shape[1]
    devices = lax.axis_size("dev")
    groups = lax.axis_size("grp")
    targets = near_list.shape[0]
    leaf_size = column_points // targets
    row_leaves = targets // (groups - 1)
    capacity = fetch_table.shape[3]
    group_index = lax.axis_index("grp")
    near_row = jnp.minimum(group_index, groups - 2)
    far_side = group_index == groups - 1
    leaf_coords = points.reshape(features, targets, leaf_size)
    leaf_weights = weights.reshape(targets, leaf_size, columns)
    requests = lax.dynamic_index_in_dim(fetch_table[:, 0], near_row, 0, keepdims=False)
    asked = lax.all_to_all(requests, "dev", split_axis=0, concat_axis=0, tiled=True)
    coords = jnp.moveaxis(jnp.take(leaf_coords, asked, axis=1), 0, 2)
    values = jnp.take(leaf_weights, asked, axis=0)
    fetched_coords = lax.all_to_all(coords, "dev", split_axis=0, concat_axis=0, tiled=True)
    fetched_values = lax.all_to_all(values, "dev", split_axis=0, concat_axis=0, tiled=True)
    flat_coords = fetched_coords.reshape(devices * capacity, features, leaf_size)
    flat_values = fetched_values.reshape(devices * capacity, leaf_size, columns)
    local_skeleton = jnp.take(points, skel_idx[0], axis=1)
    share_len = column_points // groups
    share_start = group_index * share_len
    share_proj = lax.dynamic_slice_in_dim(proj, share_start, share_len, 1)
    share_weights = lax.dynamic_slice_in_dim(weights, share_start, share_len, 0)
    partial_value = jnp.dot(
        share_proj,
        share_weights,
        preferred_element_type=jnp.float32,
        precision=lax.Precision.HIGHEST,
    )
    node_weights = lax.psum(partial_value, "grp")
    skel_coords, skel_weights = (
        lax.all_gather(local_skeleton[None], "dev", axis=0, tiled=True),
        lax.all_gather(node_weights[None], "dev", axis=0, tiled=True),
    )

    def near_work():
        slots = lax.dynamic_slice_in_dim(near_list, near_row * row_leaves, row_leaves, 0)
        leaf_numbers = near_row * row_leaves + jnp.arange(row_leaves, dtype=jnp.int32)

        def near_leaf(items):
            leaf_number, leaf_slots = items
            target = jnp.take(leaf_coords, leaf_number, axis=1)
            return kernel_sum(
                target,
                jnp.take(flat_coords, leaf_slots, axis=0),
                jnp.take(flat_values, leaf_slots, axis=0),
            )

        block = lax.map(near_leaf, (leaf_numbers, slots))
        empty = jnp.zeros((targets, leaf_size, columns), jnp.float32)
        return lax.dynamic_update_slice_in_dim(empty, block, near_row * row_leaves, 0)

    def far_work():

        def far_leaf(items):
            leaf_number, node_ids = items
            target = jnp.take(leaf_coords, leaf_number, axis=1)
            return kernel_sum(
                target,
                jnp.take(skel_coords, node_ids, axis=0),
                jnp.take(skel_weights, node_ids, axis=0),
            )

        return lax.map(far_leaf, (jnp.arange(targets, dtype=jnp.int32), far_list))

    contribution = lax.cond(far_side, far_work, near_work)
    total = lax.psum(contribution, "grp")
    return total.reshape(column_points, columns)


def solution(mesh):
    placed = (
        P(None, "dev"),
        P("dev", None),
        P(None, "dev"),
        P(None, "dev", None, None),
        P("dev", None),
        P("dev", None),
        P("dev", None),
    )
    return jax.shard_map(
        on_device, mesh=mesh, in_specs=placed, out_specs=P("dev", None), check_vma=False
    )
```

profile of v0, /device:TPU:0, one launch (start us, length us, event | category | flops | bytes accessed | tf_op | source)
XLA Modules:
  0.0 515.7 jit_solution(13828682134783458848)
XLA Ops:
  8.0 6.4 %all-to-all-start = ((s32[8,1,2]{2,1,0:T(1,128)}), s32[8,1,2]{2,1,0:T(1,128)S(1)}, u32[]{:S(2)}, u32[]{:S(2)}) async-start(s32[8,1,2]{2,1,0:T(1,128)} %copy.24), calls=%async_computation | async-start | bytes 8192 | tf_op jit(solution)/shard_map/all_to_all | solution.py:32
  27.0 4.4 all-to-all-start.1
  34.2 4.6 broadcast_select_fusion
  38.8 41.6 %all-to-all-done.1 = f32[8,2,64,512]{3,2,1,0:T(8,128)} async-done(((f32[8,2,64,512]{3,2,1,0:T(8,128)}), f32[8,2,64,512]{3,2,1,0:T(8,128)}, u32[]{:S(2)}, u32[]{:S(2)}) %all-to-all-start.1) | async-done | bytes 2097184 | tf_op jit(solution)/shard_map/all_to_all | solution.py:35
  80.4 4.6 all-to-all-start.2
  85.0 3.5 fusion.72
  88.6 43.7 %all-reduce.3.cloned.1.call-done = f32[1,256,128]{2,1,0:T(8,128)} async-done(((f32[1,256,128]{2,1,0:T(8,128)}), f32[1,256,128]{2,1,0:T(8,128)}) %all-reduce.3.cloned.1.call-update) | async-done | bytes 131088 | tf_op jit(solution)/shard_map/psum | solution.py:50
  140.3 56.1 %all_gather.6 = f32[8,64,256]{2,1,0:T(8,128)} all-gather(f32[1,64,256]{2,1,0:T(8,128)S(1)} %copy.32), channel_id=1, replica_groups=mesh['grp'=4,'dev'=8] {'dev'}, dimensions={0}, use_global_device_ids=true | all-gather | bytes 589824 | tf_op jit(solution)/shard_map/all_gather | solution.py:52
  196.5 202.2 %conditional.1 = (f32[12,512,128]{2,1,0:T(8,128)}) conditional(s32[]{:T(128)} %convert_element_type.3, (s32[]{:T(128)}, s32[12,16]{1,0:T(8,128)}, f32[8,2,64,512]{3,2,1,0:T(8,128)}, f32[8,2,512,128]{3,2,1,0:T(8,128)}, f32[64,12,512]{2,1,0:T(8,128)}) %tuple.20, (f32[64,12,512]{2,1,0:T(8,128)}, s32[12,8]{0,1:T(8,128)S(1)}, f32[8,64,256]{2,1,0:T(8,128)}, ...), branch_computations={%region_1.7_spmd, %region_6.12_spmd} | conditional | flops 9687917568 | bytes 60630836 | solution.py:86
  197.2 197.3 %while.19 = (s32[]{:T(128)}, f32[4,512,128]{2,1,0:T(8,128)}, s32[4]{0:T(128)S(1)}, f32[64,12,512]{2,1,0:T(8,128)}, s32[4,16]{1,0:T(4,128)S(1)}, /*index=5*/f32[1...) while((s32[]{:T(128)}, f32[4,512,128]{2,1,0:T(8,128)}, ...), condition=%wide.region_5.6_spmd, body=%wide.region_2.5_spmd.sunk | while | flops 9687917568 | bytes 55387260 | solution.py:69
  203.4 16.2 %fusion.106 = f32[512,16,512]{2,0,1:T(8,128)} fusion(f32[16,64,512]{2,1,0:T(8,128)S(1)} %gather_fusion.3, pred[16]{0:T(512)(128)(4,1)S(1)} %compare_and_fusion.7, f32[64,1,512]{2,1,0:T(1,128)S(1)} %constant_dynamic-slice_fusion.8, pred[]{:T(512)S(6)} %and.56), kind=kOutput, calls=%fused_computation.22.clone.1 | convolution fusion | flops 3221782528 | bytes 19005456 | tf_op jit(solution)/shard_map/cond/branch_0_fun/while/body/eval_jaxpr/dt,jds->tjs/dot_general | solution.py:9
  220.0 5.0 gather_fusion.2
  225.0 21.5 %fusion.108 = f32[4,512,128]{2,1,0:T(8,128)} fusion(f32[4,512,128]{2,1,0:T(8,128)} %get-tuple-element.303, s32[]{:T(128)} %get-tuple-element.302, f32[16,512,128]{2,1,0:T(8,128)} %gather_fusion.2, pred[16]{0:T(512)(128)(4,1)S(1)} %compare_and_fusion.7, f32[512,16,512]{2,0,1:T(8,128)} %fusion.106, f32[16,512]{1,0:T(8,128)S(1)} %multiply_reduce_fusion.5, ...), kind=kOutput, calls=%fused_computation.25.clone.1 | convolution fusion | flops 6464471040 | bytes 21269008 | tf_op jit(solution)/shard_map/cond/branch_0_fun/while/body/eval_jaxpr/tjs,jsw->tw/dot_general | solution.py:14
  252.7 16.2 %fusion.106 = f32[512,16,512]{2,0,1:T(8,128)} fusion(f32[16,64,512]{2,1,0:T(8,128)S(1)} %gather_fusion.3, pred[16]{0:T(512)(128)(4,1)S(1)} %compare_and_fusion.7, f32[64,1,512]{2,1,0:T(1,128)S(1)} %constant_dynamic-slice_fusion.8, pred[]{:T(512)S(6)} %and.56), kind=kOutput, calls=%fused_computation.22.clone.1 | convolution fusion | flops 3221782528 | bytes 19005456 | tf_op jit(solution)/shard_map/cond/branch_0_fun/while/body/eval_jaxpr/dt,jds->tjs/dot_general | solution.py:9
  269.3 5.0 gather_fusion.2
  274.3 21.5 %fusion.108 = f32[4,512,128]{2,1,0:T(8,128)} fusion(f32[4,512,128]{2,1,0:T(8,128)} %get-tuple-element.303, s32[]{:T(128)} %get-tuple-element.302, f32[16,512,128]{2,1,0:T(8,128)} %gather_fusion.2, pred[16]{0:T(512)(128)(4,1)S(1)} %compare_and_fusion.7, f32[512,16,512]{2,0,1:T(8,128)} %fusion.106, f32[16,512]{1,0:T(8,128)S(1)} %multiply_reduce_fusion.5, ...), kind=kOutput, calls=%fused_computation.25.clone.1 | convolution fusion | flops 6464471040 | bytes 21269008 | tf_op jit(solution)/shard_map/cond/branch_0_fun/while/body/eval_jaxpr/tjs,jsw->tw/dot_general | solution.py:14
  302.1 16.2 %fusion.106 = f32[512,16,512]{2,0,1:T(8,128)} fusion(f32[16,64,512]{2,1,0:T(8,128)S(1)} %gather_fusion.3, pred[16]{0:T(512)(128)(4,1)S(1)} %compare_and_fusion.7, f32[64,1,512]{2,1,0:T(1,128)S(1)} %constant_dynamic-slice_fusion.8, pred[]{:T(512)S(6)} %and.56), kind=kOutput, calls=%fused_computation.22.clone.1 | convolution fusion | flops 3221782528 | bytes 19005456 | tf_op jit(solution)/shard_map/cond/branch_0_fun/while/body/eval_jaxpr/dt,jds->tjs/dot_general | solution.py:9
  318.6 5.0 gather_fusion.2
  323.6 21.5 %fusion.108 = f32[4,512,128]{2,1,0:T(8,128)} fusion(f32[4,512,128]{2,1,0:T(8,128)} %get-tuple-element.303, s32[]{:T(128)} %get-tuple-element.302, f32[16,512,128]{2,1,0:T(8,128)} %gather_fusion.2, pred[16]{0:T(512)(128)(4,1)S(1)} %compare_and_fusion.7, f32[512,16,512]{2,0,1:T(8,128)} %fusion.106, f32[16,512]{1,0:T(8,128)S(1)} %multiply_reduce_fusion.5, ...), kind=kOutput, calls=%fused_computation.25.clone.1 | convolution fusion | flops 6464471040 | bytes 21269008 | tf_op jit(solution)/shard_map/cond/branch_0_fun/while/body/eval_jaxpr/tjs,jsw->tw/dot_general | solution.py:14
  351.4 16.2 %fusion.106 = f32[512,16,512]{2,0,1:T(8,128)} fusion(f32[16,64,512]{2,1,0:T(8,128)S(1)} %gather_fusion.3, pred[16]{0:T(512)(128)(4,1)S(1)} %compare_and_fusion.7, f32[64,1,512]{2,1,0:T(1,128)S(1)} %constant_dynamic-slice_fusion.8, pred[]{:T(512)S(6)} %and.56), kind=kOutput, calls=%fused_computation.22.clone.1 | convolution fusion | flops 3221782528 | bytes 19005456 | tf_op jit(solution)/shard_map/cond/branch_0_fun/while/body/eval_jaxpr/dt,jds->tjs/dot_general | solution.py:9
  367.9 5.0 gather_fusion.2
  372.9 21.5 %fusion.108 = f32[4,512,128]{2,1,0:T(8,128)} fusion(f32[4,512,128]{2,1,0:T(8,128)} %get-tuple-element.303, s32[]{:T(128)} %get-tuple-element.302, f32[16,512,128]{2,1,0:T(8,128)} %gather_fusion.2, pred[16]{0:T(512)(128)(4,1)S(1)} %compare_and_fusion.7, f32[512,16,512]{2,0,1:T(8,128)} %fusion.106, f32[16,512]{1,0:T(8,128)S(1)} %multiply_reduce_fusion.5, ...), kind=kOutput, calls=%fused_computation.25.clone.1 | convolution fusion | flops 6464471040 | bytes 21269008 | tf_op jit(solution)/shard_map/cond/branch_0_fun/while/body/eval_jaxpr/tjs,jsw->tw/dot_general | solution.py:14
  398.7 106.7 %all-reduce.5.cloned.1.call-done = f32[6144,128]{1,0:T(8,128)} async-done(((f32[6144,128]{1,0:T(8,128)}), f32[6144,128]{1,0:T(8,128)}) %all-reduce.5.cloned.1.call-update) | async-done | bytes 3145744 | tf_op jit(solution)/shard_map/psum | solution.py:87
  505.4 3.8 copy.80
  (77 shorter events, 48.7 us)
Async XLA Ops:
  6.5 24.8 %copy-start = (f32[6144,128]{1,0:T(8,128)S(1)}, f32[6144,128]{1,0:T(8,128)}, u32[]{:S(2)}) copy-start(f32[6144,128]{1,0:T(8,128)} %param.16) | copy-start | bytes 9437188
  8.0 11.9 %all-to-all-start = ((s32[8,1,2]{2,1,0:T(1,128)}), s32[8,1,2]{2,1,0:T(1,128)S(1)}, u32[]{:S(2)}, u32[]{:S(2)}) async-start(s32[8,1,2]{2,1,0:T(1,128)} %copy.24), calls=%async_computation | async-start | bytes 8192 | tf_op jit(solution)/shard_map/all_to_all | solution.py:32
  27.0 53.4 %all-to-all-start.1 = ((f32[8,2,64,512]{3,2,1,0:T(8,128)}), f32[8,2,64,512]{3,2,1,0:T(8,128)}, u32[]{:S(2)}, u32[]{:S(2)}) async-start(f32[8,2,64,512]{3,2,1,0:T(8,128)} %broadcast_select_fusion.1), calls=%async_computation.1 | async-start | bytes 4194304 | tf_op jit(solution)/shard_map/all_to_all | solution.py:35
  80.4 116.1 %all-to-all-start.2 = ((f32[8,2,512,128]{3,2,1,0:T(8,128)}), f32[8,2,512,128]{3,2,1,0:T(8,128)}, u32[]{:S(2)}, u32[]{:S(2)}) async-start(f32[8,2,512,128]{3,2,1,0:T(8,128)} %broadcast_select_fusion), calls=%async_computation.2 | async-start | bytes 8388608 | tf_op jit(solution)/shard_map/all_to_all | solution.py:36
  85.0 47.3 %all-reduce.3.cloned.1.call-start = ((), (), s32[]{:S(2)}) async-start(), calls=%async_computation.3 | async-start | bytes 262144 | tf_op jit(solution)/shard_map/psum | solution.py:50
  88.5 46.7 %copy-start.3 = (f32[64,6144]{1,0:T(8,128)S(1)}, f32[64,6144]{1,0:T(8,128)}, u32[]{:S(2)}) copy-start(f32[64,6144]{1,0:T(8,128)} %param.15) | copy-start | bytes 4718596
  88.5 107.9 %all-gather.2.cloned.1.call-start = ((), (), s32[]{:S(2)}) async-start(), calls=%async_computation.4 | async-start | bytes 1179648 | tf_op jit(solution)/shard_map/all_gather | solution.py:53
  132.3 5.2 %copy-start.5 = (s32[1,256]{1,0:T(1,128)S(1)}, s32[1,256]{1,0:T(1,128)}, u32[]{:S(2)}) copy-start(s32[1,256]{1,0:T(1,128)} %param.21) | copy-start | bytes 3076
  132.3 64.1 %copy-start.4 = (s32[12,8]{0,1:T(8,128)S(1)}, s32[12,8]{0,1:T(8,128)}, u32[]{:S(2)}) copy-start(s32[12,8]{0,1:T(8,128)} %param.20) | copy-start | bytes 1156
  132.3 373.1 %all-reduce.5.cloned.1.call-start = ((), (), s32[]{:S(2)}) async-start(), calls=%async_computation.5 | async-start | bytes 6291456 | tf_op jit(solution)/shard_map/psum | solution.py:87
  398.7 110.5 %copy-start.1 = (f32[6144,128]{1,0:T(8,128)S(1)}, f32[6144,128]{1,0:T(8,128)}, u32[]{:S(2)}) copy-start(f32[6144,128]{1,0:T(8,128)} %param.16) | copy-start | bytes 9437188
Sparse Core Ops, SparseCore 0:
  88.7 43.5 all-reduce.2
  133.9 39.0 all-gather.1
  398.8 106.5 all-reduce.4
where the time goes:
time: 518 us; the launch traced here: 516 us
  waiting for transfers between devices  195 us (38%)
  matrix products  154 us (30%)
  local copies, waits for them, and re-layouts  64.2 us (12%)
  blocking collectives  56.1 us (11%)
  starting transfers between devices  15.4 us (3%)
  between operations  13.2 us (3%)
  other arithmetic  9.78 us (2%)
  loops' own time  7.83 us (2%)
    psum x1, waiting for transfers between devices, on_device(): total = lax.psum(contribution, 'grp')  107 us
    dot_general x4, matrix products, kernel_sum(): return jnp.einsum('tjs,jsw->tw', kernel, values, precision=high)  86.1 us
    dot_general x4, matrix products, kernel_sum(): inner = jnp.einsum('dt,jds->tjs', target, sources, precision=high)  64.6 us
    all_gather x1, blocking collectives, on_device(): lax.all_gather(local_skeleton[None], 'dev', axis=0, tiled=True)  56.1 us
    psum x1, waiting for transfers between devices, on_device(): node_weights = lax.psum(partial_value, 'grp')  43.7 us
    all_to_all x1, waiting for transfers between devices, on_device(): lax.all_to_all(coords, 'dev', split_axis=0, concat_axis=0, tiled=True)  41.6 us
    gather x4, local copies, waits for them, and re-layouts, near_leaf(): jnp.take(flat_values, leaf_slots, axis=0)  19.9 us
  transfers between devices with their start and end apart: 6, of which 4 were waited for; matrix products, arithmetic and copies ran while one was open for 4% of the time, Pallas kernels for 0%

commit v1 on v0

--- a/solution.py
+++ b/solution.py
@@ -1,7 +1,22 @@
+import functools
 import jax
 import jax.numpy as jnp
 from jax import lax
 from jax.sharding import PartitionSpec as P
+
+
+def choose_meshes(local_x, axis_name):
+    ndev = lax.axis_size(axis_name)
+    main, frame_out = (local_x, 0)
+    while 1 << frame_out < ndev:
+        p_next = map(lambda w: (w, w ^ 1 << frame_out), range(ndev))
+        e_now = lax.ppermute(main, axis_name, perm=list(p_next))
+        main = main + e_now
+        frame_out = frame_out + 1
+    return main
+
+
+run_the_lots_all = functools.partial(choose_meshes, axis_name="grp")
 
 
 def kernel_sum(target, sources, values):
@@ -47,7 +62,7 @@
         preferred_element_type=jnp.float32,
         precision=lax.Precision.HIGHEST,
     )
-    node_weights = lax.psum(partial_value, "grp")
+    node_weights = run_the_lots_all(partial_value)
     skel_coords, skel_weights = (
         lax.all_gather(local_skeleton[None], "dev", axis=0, tiled=True),
         lax.all_gather(node_weights[None], "dev", axis=0, tiled=True),

time: 518 us -> 521 us (level)
  blocking collectives: 56.1 us -> 89 us
  waiting for transfers between devices: 195 us -> 163 us
    psum x1 -> x0, waiting for transfers between devices: 43.7 us -> none  [on_device(): node_weights = lax.psum(partial_value, 'grp')]
    all_gather x1, blocking collectives: 56.1 us -> 89 us  [on_device(): lax.all_gather(local_skeleton[None], 'dev', axis=0, tiled=True)]
    ppermute x0 -> x2, waiting for transfers between devices: none -> 7.67 us  [choose_meshes(): e_now = lax.ppermute(main, axis_name, perm=list(p_next))]
  transfers between devices with their start and end apart: 6 -> 7, of which waited for: 4 -> 5; matrix products, arithmetic and copies ran while one was open for 4% -> 4% of each run, Pallas kernels for 0% -> 0%
where the time goes in v1:
time: 521 us; the launch traced here: 519 us
  waiting for transfers between devices  163 us (31%)
  matrix products  154 us (30%)
  blocking collectives  89 us (17%)
  local copies, waits for them, and re-layouts  63.8 us (12%)
  starting transfers between devices  18.5 us (4%)
  between operations  13.5 us (3%)
  other arithmetic  10.5 us (2%)
  loops' own time  7.05 us (1%)
    psum x1, waiting for transfers between devices, on_device(): total = lax.psum(contribution, 'grp')  111 us
    all_gather x1, blocking collectives, on_device(): lax.all_gather(local_skeleton[None], 'dev', axis=0, tiled=True)  89 us
    dot_general x4, matrix products, kernel_sum(): return jnp.einsum('tjs,jsw->tw', kernel, values, precision=high)  86.1 us
    dot_general x4, matrix products, kernel_sum(): inner = jnp.einsum('dt,jds->tjs', target, sources, precision=high)  64.6 us
    all_to_all x1, waiting for transfers between devices, on_device(): lax.all_to_all(coords, 'dev', split_axis=0, concat_axis=0, tiled=True)  41.6 us
    gather x4, local copies, waits for them, and re-layouts, near_leaf(): jnp.take(flat_values, leaf_slots, axis=0)  19.9 us
  transfers between devices with their start and end apart: 7, of which 5 were waited for; matrix products, arithmetic and copies ran while one was open for 4% of the time, Pallas kernels for 0%

profile of v1, /device:TPU:0, one launch (start us, length us, event | category | flops | bytes accessed | tf_op | source)
XLA Modules:
  0.0 518.9 jit_solution(11640831129942706588)
XLA Ops:
  8.0 6.4 %all-to-all-start = ((s32[8,1,2]{2,1,0:T(1,128)}), s32[8,1,2]{2,1,0:T(1,128)S(1)}, u32[]{:S(2)}, u32[]{:S(2)}) async-start(s32[8,1,2]{2,1,0:T(1,128)} %copy.24), calls=%async_computation | async-start | bytes 8192 | tf_op jit(solution)/shard_map/all_to_all | solution.py:47
  27.0 4.4 all-to-all-start.1
  34.2 4.6 broadcast_select_fusion
  38.8 41.6 %all-to-all-done.1 = f32[8,2,64,512]{3,2,1,0:T(8,128)} async-done(((f32[8,2,64,512]{3,2,1,0:T(8,128)}), f32[8,2,64,512]{3,2,1,0:T(8,128)}, u32[]{:S(2)}, u32[]{:S(2)}) %all-to-all-start.1) | async-done | bytes 2097184 | tf_op jit(solution)/shard_map/all_to_all | solution.py:50
  80.4 4.6 all-to-all-start.2
  89.4 4.2 collective-permute-done
  95.2 3.4 collective-permute-done.1
  107.4 89.0 %all_gather.6 = f32[8,64,256]{2,1,0:T(8,128)} all-gather(f32[1,64,256]{2,1,0:T(8,128)S(1)} %copy.32), channel_id=1, replica_groups=mesh['grp'=4,'dev'=8] {'dev'}, dimensions={0}, use_global_device_ids=true | all-gather | bytes 589824 | tf_op jit(solution)/shard_map/all_gather | solution.py:67
  196.5 201.0 %conditional.1 = (f32[12,512,128]{2,1,0:T(8,128)}) conditional(s32[]{:T(128)} %convert_element_type.3, (s32[]{:T(128)}, s32[12,16]{1,0:T(8,128)}, f32[8,2,64,512]{3,2,1,0:T(8,128)}, f32[8,2,512,128]{3,2,1,0:T(8,128)}, f32[64,12,512]{2,1,0:T(8,128)}) %tuple.20, (f32[64,12,512]{2,1,0:T(8,128)}, s32[12,8]{0,1:T(8,128)S(1)}, f32[8,64,256]{2,1,0:T(8,128)}, ...), branch_computations={%region_0.6_spmd, %region_5.11_spmd} | conditional | flops 9687917568 | bytes 60630836 | solution.py:101
  197.2 196.1 %while.19 = (s32[]{:T(128)}, f32[4,512,128]{2,1,0:T(8,128)}, s32[4]{0:T(128)S(1)}, f32[64,12,512]{2,1,0:T(8,128)}, s32[4,16]{1,0:T(4,128)S(1)}, /*index=5*/f32[1...) while((s32[]{:T(128)}, f32[4,512,128]{2,1,0:T(8,128)}, ...), condition=%wide.region_4.5_spmd, body=%wide.region_1.4_spmd.sunk | while | flops 9687917568 | bytes 55387260 | solution.py:84
  203.1 16.2 %fusion.103 = f32[512,16,512]{2,0,1:T(8,128)} fusion(f32[16,64,512]{2,1,0:T(8,128)S(1)} %gather_fusion.3, pred[16]{0:T(512)(128)(4,1)S(1)} %compare_and_fusion.7, f32[64,1,512]{2,1,0:T(1,128)S(1)} %constant_dynamic-slice_fusion.8, pred[]{:T(512)S(6)} %and.56), kind=kOutput, calls=%fused_computation.22.clone.1 | convolution fusion | flops 3221782528 | bytes 19005456 | tf_op jit(solution)/shard_map/cond/branch_0_fun/while/body/eval_jaxpr/dt,jds->tjs/dot_general | solution.py:24
  219.7 5.0 gather_fusion.2
  224.7 21.5 %fusion.105 = f32[4,512,128]{2,1,0:T(8,128)} fusion(f32[4,512,128]{2,1,0:T(8,128)} %get-tuple-element.303, s32[]{:T(128)} %get-tuple-element.302, f32[16,512,128]{2,1,0:T(8,128)} %gather_fusion.2, pred[16]{0:T(512)(128)(4,1)S(1)} %compare_and_fusion.7, f32[512,16,512]{2,0,1:T(8,128)} %fusion.103, f32[16,512]{1,0:T(8,128)S(1)} %multiply_reduce_fusion.5, ...), kind=kOutput, calls=%fused_computation.25.clone.1 | convolution fusion | flops 6464471040 | bytes 21269008 | tf_op jit(solution)/shard_map/cond/branch_0_fun/while/body/eval_jaxpr/tjs,jsw->tw/dot_general | solution.py:29
  252.1 16.2 %fusion.103 = f32[512,16,512]{2,0,1:T(8,128)} fusion(f32[16,64,512]{2,1,0:T(8,128)S(1)} %gather_fusion.3, pred[16]{0:T(512)(128)(4,1)S(1)} %compare_and_fusion.7, f32[64,1,512]{2,1,0:T(1,128)S(1)} %constant_dynamic-slice_fusion.8, pred[]{:T(512)S(6)} %and.56), kind=kOutput, calls=%fused_computation.22.clone.1 | convolution fusion | flops 3221782528 | bytes 19005456 | tf_op jit(solution)/shard_map/cond/branch_0_fun/while/body/eval_jaxpr/dt,jds->tjs/dot_general | solution.py:24
  268.7 5.0 gather_fusion.2
  273.7 21.5 %fusion.105 = f32[4,512,128]{2,1,0:T(8,128)} fusion(f32[4,512,128]{2,1,0:T(8,128)} %get-tuple-element.303, s32[]{:T(128)} %get-tuple-element.302, f32[16,512,128]{2,1,0:T(8,128)} %gather_fusion.2, pred[16]{0:T(512)(128)(4,1)S(1)} %compare_and_fusion.7, f32[512,16,512]{2,0,1:T(8,128)} %fusion.103, f32[16,512]{1,0:T(8,128)S(1)} %multiply_reduce_fusion.5, ...), kind=kOutput, calls=%fused_computation.25.clone.1 | convolution fusion | flops 6464471040 | bytes 21269008 | tf_op jit(solution)/shard_map/cond/branch_0_fun/while/body/eval_jaxpr/tjs,jsw->tw/dot_general | solution.py:29
  301.2 16.2 %fusion.103 = f32[512,16,512]{2,0,1:T(8,128)} fusion(f32[16,64,512]{2,1,0:T(8,128)S(1)} %gather_fusion.3, pred[16]{0:T(512)(128)(4,1)S(1)} %compare_and_fusion.7, f32[64,1,512]{2,1,0:T(1,128)S(1)} %constant_dynamic-slice_fusion.8, pred[]{:T(512)S(6)} %and.56), kind=kOutput, calls=%fused_computation.22.clone.1 | convolution fusion | flops 3221782528 | bytes 19005456 | tf_op jit(solution)/shard_map/cond/branch_0_fun/while/body/eval_jaxpr/dt,jds->tjs/dot_general | solution.py:24
  317.7 5.0 gather_fusion.2
  322.7 21.5 %fusion.105 = f32[4,512,128]{2,1,0:T(8,128)} fusion(f32[4,512,128]{2,1,0:T(8,128)} %get-tuple-element.303, s32[]{:T(128)} %get-tuple-element.302, f32[16,512,128]{2,1,0:T(8,128)} %gather_fusion.2, pred[16]{0:T(512)(128)(4,1)S(1)} %compare_and_fusion.7, f32[512,16,512]{2,0,1:T(8,128)} %fusion.103, f32[16,512]{1,0:T(8,128)S(1)} %multiply_reduce_fusion.5, ...), kind=kOutput, calls=%fused_computation.25.clone.1 | convolution fusion | flops 6464471040 | bytes 21269008 | tf_op jit(solution)/shard_map/cond/branch_0_fun/while/body/eval_jaxpr/tjs,jsw->tw/dot_general | solution.py:29
  350.2 16.2 %fusion.103 = f32[512,16,512]{2,0,1:T(8,128)} fusion(f32[16,64,512]{2,1,0:T(8,128)S(1)} %gather_fusion.3, pred[16]{0:T(512)(128)(4,1)S(1)} %compare_and_fusion.7, f32[64,1,512]{2,1,0:T(1,128)S(1)} %constant_dynamic-slice_fusion.8, pred[]{:T(512)S(6)} %and.56), kind=kOutput, calls=%fused_computation.22.clone.1 | convolution fusion | flops 3221782528 | bytes 19005456 | tf_op jit(solution)/shard_map/cond/branch_0_fun/while/body/eval_jaxpr/dt,jds->tjs/dot_general | solution.py:24
  366.8 5.0 gather_fusion.2
  371.7 21.5 %fusion.105 = f32[4,512,128]{2,1,0:T(8,128)} fusion(f32[4,512,128]{2,1,0:T(8,128)} %get-tuple-element.303, s32[]{:T(128)} %get-tuple-element.302, f32[16,512,128]{2,1,0:T(8,128)} %gather_fusion.2, pred[16]{0:T(512)(128)(4,1)S(1)} %compare_and_fusion.7, f32[512,16,512]{2,0,1:T(8,128)} %fusion.103, f32[16,512]{1,0:T(8,128)S(1)} %multiply_reduce_fusion.5, ...), kind=kOutput, calls=%fused_computation.25.clone.1 | convolution fusion | flops 6464471040 | bytes 21269008 | tf_op jit(solution)/shard_map/cond/branch_0_fun/while/body/eval_jaxpr/tjs,jsw->tw/dot_general | solution.py:29
  397.5 110.7 %all-reduce.2.cloned.1.call-done = f32[6144,128]{1,0:T(8,128)} async-done(((f32[6144,128]{1,0:T(8,128)}), f32[6144,128]{1,0:T(8,128)}) %all-reduce.2.cloned.1.call-update) | async-done | bytes 3145744 | tf_op jit(solution)/shard_map/psum | solution.py:102
  508.3 3.8 copy.79
  (80 shorter events, 55.0 us)
Async XLA Ops:
  6.5 24.8 %copy-start = (f32[6144,128]{1,0:T(8,128)S(1)}, f32[6144,128]{1,0:T(8,128)}, u32[]{:S(2)}) copy-start(f32[6144,128]{1,0:T(8,128)} %param.16) | copy-start | bytes 9437188
  8.0 11.9 %all-to-all-start = ((s32[8,1,2]{2,1,0:T(1,128)}), s32[8,1,2]{2,1,0:T(1,128)S(1)}, u32[]{:S(2)}, u32[]{:S(2)}) async-start(s32[8,1,2]{2,1,0:T(1,128)} %copy.24), calls=%async_computation | async-start | bytes 8192 | tf_op jit(solution)/shard_map/all_to_all | solution.py:47
  27.0 53.4 %all-to-all-start.1 = ((f32[8,2,64,512]{3,2,1,0:T(8,128)}), f32[8,2,64,512]{3,2,1,0:T(8,128)}, u32[]{:S(2)}, u32[]{:S(2)}) async-start(f32[8,2,64,512]{3,2,1,0:T(8,128)} %broadcast_select_fusion.1), calls=%async_computation.1 | async-start | bytes 4194304 | tf_op jit(solution)/shard_map/all_to_all | solution.py:50
  80.4 116.0 %all-to-all-start.2 = ((f32[8,2,512,128]{3,2,1,0:T(8,128)}), f32[8,2,512,128]{3,2,1,0:T(8,128)}, u32[]{:S(2)}, u32[]{:S(2)}) async-start(f32[8,2,512,128]{3,2,1,0:T(8,128)} %broadcast_select_fusion), calls=%async_computation.2 | async-start | bytes 8388608 | tf_op jit(solution)/shard_map/all_to_all | solution.py:51
  85.0 111.5 %all-gather.3.cloned.1.call-start = ((), (), s32[]{:S(2)}) async-start(), calls=%async_computation.4 | async-start | bytes 1179648 | tf_op jit(solution)/shard_map/all_gather | solution.py:68
  87.8 14.5 %copy-start.3 = (f32[64,6144]{1,0:T(8,128)S(1)}, f32[64,6144]{1,0:T(8,128)}, u32[]{:S(2)}) copy-start(f32[64,6144]{1,0:T(8,128)} %param.15) | copy-start | bytes 4718596
  87.9 5.8 %collective-permute-start = (f32[256,128]{1,0:T(8,128)S(1)}, f32[256,128]{1,0:T(8,128)S(1)}, u32[]{:S(2)}, u32[]{:S(2)}) collective-permute-start(f32[256,128]{1,0:T(8,128)S(1)} %fusion.70), channel_id=1, source_target_pairs={{0,8},{8,0},{16,24},{24,16},{1,9},{9,1},{17,25},{25,17},{2,10},{10... | collective-permute-start | bytes 393224 | tf_op jit(solution)/shard_map/ppermute | solution.py:13
  93.7 5.0 collective-permute-start.1
  99.4 5.2 %copy-start.5 = (s32[1,256]{1,0:T(1,128)S(1)}, s32[1,256]{1,0:T(1,128)}, u32[]{:S(2)}) copy-start(s32[1,256]{1,0:T(1,128)} %param.21) | copy-start | bytes 3076
  99.4 97.0 %copy-start.4 = (s32[12,8]{0,1:T(8,128)S(1)}, s32[12,8]{0,1:T(8,128)}, u32[]{:S(2)}) copy-start(s32[12,8]{0,1:T(8,128)} %param.20) | copy-start | bytes 1156
  99.4 408.8 %all-reduce.2.cloned.1.call-start = ((), (), s32[]{:S(2)}) async-start(), calls=%async_computation.3 | async-start | bytes 6291456 | tf_op jit(solution)/shard_map/psum | solution.py:102
  397.5 114.5 %copy-start.1 = (f32[6144,128]{1,0:T(8,128)S(1)}, f32[6144,128]{1,0:T(8,128)}, u32[]{:S(2)}) copy-start(f32[6144,128]{1,0:T(8,128)} %param.16) | copy-start | bytes 9437188
Sparse Core Ops, SparseCore 0:
  99.5 31.7 all-gather.2
  397.6 110.5 all-reduce.1
